TPU v7x, 32 devices: a whole 2x2x4 slice. The times are simulated.
32 devices in a mesh: grp: 4 (over y, x), tp: 8 (over z, core).
Axes of the slice: x: 2, y: 2, z: 4, core: 2. Of those that a mesh axis runs over, the one named last changes fastest.
Arguments:
- batch_sizes: int32 [4], P('grp'), may hold values from 1 to 16
- seq_lens: int32 [4, 16], P('grp'), may hold values from 1 to 2048
- page_table: int32 [4, 16, 128], P('grp', None, 'tp'), may hold values from 0 to 255, as said below
- queries: bfloat16 [4, 16, 4096], P('grp', None, 'tp'), may hold values from -4 to 14
- kv_pool: bfloat16 [4, 2048, 16, 1024], P('grp', 'tp'), may hold values from -7 to 7
- new_kv: bfloat16 [4, 16, 1024], P('grp'), may hold values from -6 to 6
- out_weight: bfloat16 [4096, 2880], P('tp', 'grp'), may hold values from -0.375 to 0.375
Outputs:
- mixed: float32 [4, 16, 2880], P('grp')
Inputs may be any that keep to these rules, and one draw needn't show every extreme that they name: `batch_sizes`: slots below a group's batch size are live; the others are empty and their outputs are zero. `seq_lens`: entries of empty slots are drawn but unused. `page_table`: for every group g and every t, the entries [g, :, t * 16 to (t + 1) * 16 - 1] are a permutation of 0 to 255.
All inputs are finite; a program needn't handle non-finite values.
Results may differ from a plain program's by a relative error of at most 0.007.
Values may be sent and summed in bfloat16 or wider, within the bound.
A program may use at most 64 MiB of HBM per device.

v0:
```python
import jax
import jax.numpy as jnp
from jax import lax
from jax.sharding import PartitionSpec as P

HEADS = 64
KV_HEADS = 8
HD = 64
SLOT_BLOCK = 2
PRECISE = lax.Precision.HIGHEST
NEG_BIG = -1e30


def attend_slots(query_rows, page_blocks, lengths, tp_index, tp_count, kv_heads):
    slot_count, page_count, page_len, row_width = page_blocks.shape
    head_dim = row_width // (2 * kv_heads)
    head_count = query_rows.shape[1] // head_dim
    group_size = head_count // kv_heads
    token_count = page_count * page_len
    token_rows = page_blocks.reshape(slot_count, token_count, row_width)
    key_rows = token_rows[:, :, : row_width // 2].reshape(
        slot_count, token_count, kv_heads, head_dim
    )
    value_rows = token_rows[:, :, row_width // 2 :].reshape(
        slot_count, token_count, kv_heads, head_dim
    )
    grouped = query_rows.reshape(slot_count, kv_heads, group_size, head_dim)
    scores = jnp.einsum("skgd,stkd->skgt", grouped, key_rows, preferred_element_type=jnp.float32)
    scores = scores * head_dim ** (-0.5)
    page_index = lax.broadcasted_iota(jnp.int32, (page_count, page_len), 0)
    token_index = lax.broadcasted_iota(jnp.int32, (page_count, page_len), 1)
    position = ((page_index * tp_count + tp_index) * page_len + token_index).reshape(token_count)
    valid_mask = (position[None, :] < lengths[:, None])[:, None, None, :]
    scores = jnp.where(valid_mask, scores, NEG_BIG)
    top_score = jnp.max(scores, axis=3)
    weights = jnp.where(valid_mask, jnp.exp(scores - top_score[..., None]), 0.0)
    weight_sum = jnp.sum(weights, axis=3)
    weighted = jnp.einsum(
        "skgt,stkd->skgd",
        weights.astype(jnp.bfloat16),
        value_rows,
        preferred_element_type=jnp.float32,
    )
    return (
        weighted.reshape(slot_count, head_count * head_dim),
        top_score.reshape(slot_count, head_count),
        weight_sum.reshape(slot_count, head_count),
    )


def local(batch_sizes, seq_lens, page_table, queries, kv_pool, new_kv, out_weight):
    tp_count = lax.axis_size("tp")
    tp_index = lax.axis_index("tp")
    gathered = lax.all_gather(queries, "tp", axis=2, tiled=True)[0]
    kv_pages = kv_pool[0]
    page_ids = page_table[0]
    lengths = seq_lens[0]
    live_count = batch_sizes[0]
    slot_count, full_width = gathered.shape
    head_dim = HD
    head_count = HEADS
    slot_order = jnp.arange(slot_count, dtype=jnp.int32)

    def local_block(block_index, state):
        first_slot = block_index * SLOT_BLOCK
        query_rows = lax.dynamic_slice_in_dim(gathered, first_slot, SLOT_BLOCK, 0)
        block_ids = lax.dynamic_slice_in_dim(page_ids, first_slot, SLOT_BLOCK, 0)
        block_lengths = lax.dynamic_slice_in_dim(lengths, first_slot, SLOT_BLOCK, 0)
        block_slots = first_slot + jnp.arange(SLOT_BLOCK, dtype=jnp.int32)
        block_lengths = jnp.where(block_slots < live_count, block_lengths, 0)
        pieces = attend_slots(
            query_rows, kv_pages[block_ids], block_lengths, tp_index, tp_count, KV_HEADS
        )
        return tuple(
            (
                lax.dynamic_update_slice_in_dim(whole, piece, first_slot, 0)
                for whole, piece in zip(state, pieces)
            )
        )

    start_state = (
        jnp.zeros((slot_count, full_width), jnp.float32),
        jnp.full((slot_count, head_count), NEG_BIG, jnp.float32),
        jnp.zeros((slot_count, head_count), jnp.float32),
    )
    block_total = (live_count + SLOT_BLOCK - 1) // SLOT_BLOCK
    weighted, top_score, weight_sum = lax.fori_loop(0, block_total, local_block, start_state)
    own_heads = head_count // tp_count
    own_width = own_heads * head_dim
    shard_weighted, shard_top, shard_sum = (
        lax.all_to_all(weighted[None], "tp", split_axis=2, concat_axis=0, tiled=True),
        lax.all_to_all(top_score[None], "tp", split_axis=2, concat_axis=0, tiled=True),
        lax.all_to_all(weight_sum[None], "tp", split_axis=2, concat_axis=0, tiled=True),
    )
    part_top = jnp.max(shard_top, axis=0)
    shard_rescale = jnp.exp(shard_top - part_top[None])
    part_weighted = jnp.sum(shard_weighted * jnp.repeat(shard_rescale, head_dim, axis=-1), axis=0)
    part_sum = jnp.sum(shard_sum * shard_rescale, axis=0)
    fresh_rows = new_kv[0].astype(jnp.float32)
    kv_width = KV_HEADS * head_dim
    new_keys = fresh_rows[:, :kv_width].reshape(slot_count, KV_HEADS, head_dim)
    new_values = fresh_rows[:, kv_width:].reshape(slot_count, KV_HEADS, head_dim)
    head_ids = tp_index * own_heads + jnp.arange(own_heads, dtype=jnp.int32)
    head_map = (
        head_ids[:, None] // (head_count // KV_HEADS)
        == jnp.arange(KV_HEADS, dtype=jnp.int32)[None, :]
    ).astype(jnp.float32)
    own_keys = jnp.einsum("jk,skd->sjd", head_map, new_keys, precision=PRECISE)
    own_values = jnp.einsum("jk,skd->sjd", head_map, new_values, precision=PRECISE)
    own_queries = queries[0].astype(jnp.float32).reshape(slot_count, own_heads, head_dim)
    self_score = jnp.sum(own_queries * own_keys, axis=-1) * head_dim ** (-0.5)
    final_top = jnp.maximum(part_top, self_score)
    cache_rescale = jnp.exp(part_top - final_top)
    self_rescale = jnp.exp(self_score - final_top)
    numerator = part_weighted.reshape(slot_count, own_heads, head_dim) * cache_rescale[..., None]
    numerator = numerator + own_values * self_rescale[..., None]
    denominator = part_sum * cache_rescale + self_rescale
    attended = (numerator / denominator[..., None]).reshape(slot_count, own_width)
    attended = jnp.where((slot_order < live_count)[:, None], attended, 0.0).astype(jnp.bfloat16)
    projected = jnp.dot(
        attended,
        lax.all_gather(out_weight, "grp", axis=1, tiled=True),
        preferred_element_type=jnp.float32,
    )
    mixed = lax.psum(projected, "tp")
    return mixed[None]


def solution(mesh):
    return jax.shard_map(
        local,
        mesh=mesh,
        in_specs=(
            P("grp"),
            P("grp", None),
            P("grp", None, "tp"),
            P("grp", None, "tp"),
            P("grp", "tp", None, None),
            P("grp", None, None),
            P("tp", "grp"),
        ),
        out_specs=P("grp", None, None),
        check_vma=False,
    )
```

profile of v0, /device:TPU:0, one launch (start us, length us, event | category | flops | bytes accessed | tf_op | source)
XLA Modules:
  0.0 214.4 jit_solution(14500293375372935720)
XLA Ops:
  6.5 0.7 all-gather.2.cloned.1.call-update
  7.9 15.9 %all_gather.6 = bf16[1,16,4096]{2,1,0:T(8,128)(2,1)S(1)} all-gather(bf16[1,16,512]{2,1,0:T(8,128)(2,1)} %param.12), channel_id=1, replica_groups=mesh['grp'=4,'tp'=8] {'tp'}, dimensions={2}, use_global_device_ids=true | all-gather | bytes 147456 | tf_op jit(solution)/shard_map/all_gather | solution.py:54
  23.9 65.7 %while.14 = (s32[]{:T(128)}, f32[16,4096]{1,0:T(8,128)S(1)}, f32[16,64]{1,0:T(8,128)S(1)}, f32[16,64]{1,0:T(8,128)S(1)}, s32[]{:T(128)}, /*index=5*/s32[]{:T(128...) while((s32[]{:T(128)}, f32[16,4096]{1,0:T(8,128)S(1)}, ...), condition=%wide.region_3.4_spmd, body=%wide.region_0.3_spmd.sunk | while | flops 8685212 | bytes 7998579 | solution.py:87
  24.0 1.4 compare_select_fusion.8
  26.4 4.0 %gather_fusion = bf16[32,16,1024]{2,1,0:T(8,128)(2,1)S(1)} fusion(bf16[256,16,1024]{2,1,0:T(8,128)(2,1)} %get-tuple-element.223, s32[1024]{0:T(1024)S(1)} %pad_clamp_fusion.2), kind=kCustom, calls=%fused_computation.clone.1 | custom fusion | bytes 2097280 | tf_op jit(solution)/shard_map/while/body/gather | solution.py:72
  32.1 1.4 compare_select_fusion.8
  34.5 4.5 %gather_fusion = bf16[32,16,1024]{2,1,0:T(8,128)(2,1)S(1)} fusion(bf16[256,16,1024]{2,1,0:T(8,128)(2,1)} %get-tuple-element.223, s32[1024]{0:T(1024)S(1)} %pad_clamp_fusion.2), kind=kCustom, calls=%fused_computation.clone.1 | custom fusion | bytes 2097280 | tf_op jit(solution)/shard_map/while/body/gather | solution.py:72
  40.8 1.4 compare_select_fusion.8
  43.2 4.0 %gather_fusion = bf16[32,16,1024]{2,1,0:T(8,128)(2,1)S(1)} fusion(bf16[256,16,1024]{2,1,0:T(8,128)(2,1)} %get-tuple-element.223, s32[1024]{0:T(1024)S(1)} %pad_clamp_fusion.2), kind=kCustom, calls=%fused_computation.clone.1 | custom fusion | bytes 2097280 | tf_op jit(solution)/shard_map/while/body/gather | solution.py:72
  48.9 1.4 compare_select_fusion.8
  51.3 4.0 %gather_fusion = bf16[32,16,1024]{2,1,0:T(8,128)(2,1)S(1)} fusion(bf16[256,16,1024]{2,1,0:T(8,128)(2,1)} %get-tuple-element.223, s32[1024]{0:T(1024)S(1)} %pad_clamp_fusion.2), kind=kCustom, calls=%fused_computation.clone.1 | custom fusion | bytes 2097280 | tf_op jit(solution)/shard_map/while/body/gather | solution.py:72
  57.0 1.4 compare_select_fusion.8
  59.5 4.0 %gather_fusion = bf16[32,16,1024]{2,1,0:T(8,128)(2,1)S(1)} fusion(bf16[256,16,1024]{2,1,0:T(8,128)(2,1)} %get-tuple-element.223, s32[1024]{0:T(1024)S(1)} %pad_clamp_fusion.2), kind=kCustom, calls=%fused_computation.clone.1 | custom fusion | bytes 2097280 | tf_op jit(solution)/shard_map/while/body/gather | solution.py:72
  65.2 1.4 compare_select_fusion.8
  67.6 4.0 %gather_fusion = bf16[32,16,1024]{2,1,0:T(8,128)(2,1)S(1)} fusion(bf16[256,16,1024]{2,1,0:T(8,128)(2,1)} %get-tuple-element.223, s32[1024]{0:T(1024)S(1)} %pad_clamp_fusion.2), kind=kCustom, calls=%fused_computation.clone.1 | custom fusion | bytes 2097280 | tf_op jit(solution)/shard_map/while/body/gather | solution.py:72
  73.3 1.4 compare_select_fusion.8
  75.7 4.0 %gather_fusion = bf16[32,16,1024]{2,1,0:T(8,128)(2,1)S(1)} fusion(bf16[256,16,1024]{2,1,0:T(8,128)(2,1)} %get-tuple-element.223, s32[1024]{0:T(1024)S(1)} %pad_clamp_fusion.2), kind=kCustom, calls=%fused_computation.clone.1 | custom fusion | bytes 2097280 | tf_op jit(solution)/shard_map/while/body/gather | solution.py:72
  81.5 1.4 compare_select_fusion.8
  83.9 4.0 %gather_fusion = bf16[32,16,1024]{2,1,0:T(8,128)(2,1)S(1)} fusion(bf16[256,16,1024]{2,1,0:T(8,128)(2,1)} %get-tuple-element.223, s32[1024]{0:T(1024)S(1)} %pad_clamp_fusion.2), kind=kCustom, calls=%fused_computation.clone.1 | custom fusion | bytes 2097280 | tf_op jit(solution)/shard_map/while/body/gather | solution.py:72
  91.6 4.6 %all-to-all-start.1 = ((f32[8,1,128]{2,1,0:T(1,128)}), f32[8,1,128]{2,1,0:T(1,128)S(1)}, u32[]{:S(2)}, u32[]{:S(2)}) async-start(f32[8,1,128]{2,1,0:T(1,128)} %reshape.169), calls=%async_computation.1 | async-start | bytes 8192 | tf_op jit(solution)/shard_map/all_to_all | solution.py:92
  96.4 0.7 reduce.3
  97.9 3.9 %all-to-all-done.1 = f32[8,1,128]{2,1,0:T(1,128)S(1)} async-done(((f32[8,1,128]{2,1,0:T(1,128)}), f32[8,1,128]{2,1,0:T(1,128)S(1)}, u32[]{:S(2)}, u32[]{:S(2)}) %all-to-all-start.1) | async-done | bytes 4128 | tf_op jit(solution)/shard_map/all_to_all | solution.py:92
  101.8 3.3 %all-to-all-start.2 = ((f32[8,1,128]{2,1,0:T(1,128)}), f32[8,1,128]{2,1,0:T(1,128)S(1)}, u32[]{:S(2)}, u32[]{:S(2)}) async-start(f32[8,1,128]{2,1,0:T(1,128)} %reshape.171), calls=%async_computation.2 | async-start | bytes 8192 | tf_op jit(solution)/shard_map/all_to_all | solution.py:93
  106.0 19.3 %reduce.1 = f32[4096,16]{1,0:T(8,128)} reduce(f32[4096,1,16]{2,1,0:T(1,128)S(1)} %bitcast.84, f32[]{:T(128)} %broadcast.132), dimensions={1}, to_apply=%bitcast.54.reduce_sub_computation | reduce | bytes 524292
  125.3 3.0 %reshape.167 = f32[8,1,8192]{2,1,0:T(1,128)} reshape(f32[4096,16]{1,0:T(8,128)} %reduce.1) | data formatting | bytes 524288
  128.3 5.0 %all-to-all-start = ((f32[8,1,8192]{2,1,0:T(1,128)}), f32[8,1,8192]{2,1,0:T(1,128)S(1)}, u32[]{:S(2)}, u32[]{:S(2)}) async-start(f32[8,1,8192]{2,1,0:T(1,128)} %reshape.167), calls=%async_computation | async-start | bytes 524288 | tf_op jit(solution)/shard_map/all_to_all | solution.py:91
  135.5 7.5 %all-to-all-done = f32[8,1,8192]{2,1,0:T(1,128)S(1)} async-done(((f32[8,1,8192]{2,1,0:T(1,128)}), f32[8,1,8192]{2,1,0:T(1,128)S(1)}, u32[]{:S(2)}, u32[]{:S(2)}) %all-to-all-start) | async-done | bytes 262176 | tf_op jit(solution)/shard_map/all_to_all | solution.py:91
  143.1 1.2 reduce.2
  144.3 3.9 %reshape.168 = f32[4096,1,16]{2,1,0:T(1,128)S(1)} reshape(f32[8,8192]{1,0:T(8,128)S(1)} %reduce.2) | data formatting | bytes 524288
  149.0 3.4 %convolution_bitcast_fusion = f32[1,16,2880]{2,1,0:T(8,128)} fusion(bf16[512,2880]{0,1:T(8,128)(2,1)} %all-gather.2.cloned.1.call-done, bf16[16,512]{1,0:T(8,128)(2,1)S(1)} %reshape.153, pred[16]{0:T(512)(128)(4,1)S(1)} %iota_compare_fusion.1), kind=kOutput, calls=%fused_computation.22 | convolution fusion | flops 47194112 | bytes 3149840 | tf_op jit(solution)/shard_map/dot_general | solution.py:120
  152.4 53.6 %all-reduce.2.cloned.1.call-done = f32[1,16,2880]{2,1,0:T(8,128)} async-done(((f32[1,16,2880]{2,1,0:T(8,128)}), f32[1,16,2880]{2,1,0:T(8,128)}) %all-reduce.2.cloned.1.call-update) | async-done | bytes 184336 | tf_op jit(solution)/shard_map/psum | solution.py:125
  206.0 1.6 copy.58
  (201 shorter events, 28.2 us)
Async XLA Ops:
  6.5 142.4 %all-gather.2.cloned.1.call-start = ((), (), s32[]{:S(2)}) async-start(), calls=%async_computation.3 | async-start | bytes 3686400 | tf_op jit(solution)/shard_map/all_gather | solution.py:122
  23.9 72.3 %copy-start.1 = (bf16[1,16,1024]{2,1,0:T(8,128)(2,1)S(1)}, bf16[1,16,1024]{2,1,0:T(8,128)(2,1)}, u32[]{:S(2)}) copy-start(bf16[1,16,1024]{2,1,0:T(8,128)(2,1)} %param.14) | copy-start | bytes 98308
  23.9 72.3 %copy-start = (bf16[1,16,512]{2,1,0:T(8,128)(2,1)S(1)}, bf16[1,16,512]{2,1,0:T(8,128)(2,1)}, u32[]{:S(2)}) copy-start(bf16[1,16,512]{2,1,0:T(8,128)(2,1)} %param.12) | copy-start | bytes 49156
  91.6 10.2 %all-to-all-start.1 = ((f32[8,1,128]{2,1,0:T(1,128)}), f32[8,1,128]{2,1,0:T(1,128)S(1)}, u32[]{:S(2)}, u32[]{:S(2)}) async-start(f32[8,1,128]{2,1,0:T(1,128)} %reshape.169), calls=%async_computation.1 | async-start | bytes 8192 | tf_op jit(solution)/shard_map/all_to_all | solution.py:92
  101.8 26.5 %all-to-all-start.2 = ((f32[8,1,128]{2,1,0:T(1,128)}), f32[8,1,128]{2,1,0:T(1,128)S(1)}, u32[]{:S(2)}, u32[]{:S(2)}) async-start(f32[8,1,128]{2,1,0:T(1,128)} %reshape.171), calls=%async_computation.2 | async-start | bytes 8192 | tf_op jit(solution)/shard_map/all_to_all | solution.py:93
  128.3 14.7 %all-to-all-start = ((f32[8,1,8192]{2,1,0:T(1,128)}), f32[8,1,8192]{2,1,0:T(1,128)S(1)}, u32[]{:S(2)}, u32[]{:S(2)}) async-start(f32[8,1,8192]{2,1,0:T(1,128)} %reshape.167), calls=%async_computation | async-start | bytes 524288 | tf_op jit(solution)/shard_map/all_to_all | solution.py:91
  133.4 72.6 %all-reduce.2.cloned.1.call-start = ((), (), s32[]{:S(2)}) async-start(), calls=%async_computation.4 | async-start | bytes 376832 | tf_op jit(solution)/shard_map/psum | solution.py:125
Sparse Core Ops, SparseCore 0:
  9.2 44.9 all-gather.1
  152.5 53.4 all-reduce.1
where the time goes:
time: 216 us; the launch traced here: 214 us
  waiting for transfers between devices  65.8 us (30%)
  local copies, waits for them, and re-layouts  53.4 us (25%)
  other arithmetic  42.9 us (20%)
  blocking collectives  15.9 us (7%)
  between operations  14.3 us (7%)
  starting transfers between devices  13.2 us (6%)
  matrix products  8.29 us (4%)
    psum x1, waiting for transfers between devices, local(): mixed = lax.psum(projected, 'tp')  53.6 us
    gather x8, local copies, waits for them, and re-layouts, local_block(): kv_pages[block_ids]  32.4 us
    unnamed x3, other arithmetic  20.7 us
    all_gather x1, blocking collectives, local(): gathered = lax.all_gather(queries, 'tp', axis=2, tiled=True)[0]  15.9 us
    select_n x8, other arithmetic, local_block(): block_lengths = jnp.where(block_slots < live_count, block_lengths, 0)  11 us
    unnamed x12, local copies, waits for them, and re-layouts  10.6 us
    all_to_all x1, waiting for transfers between devices, local(): lax.all_to_all(weighted[None], 'tp', split_axis=2, concat_axis=0, tiled=T...  7.53 us
    select_n x8, other arithmetic, local_block(): kv_pages[block_ids]  5.57 us
  transfers between devices with their start and end apart: 5, of which 3 were waited for; matrix products, arithmetic and copies ran while one was open for 46% of the time, Pallas kernels for 0%

commit v1 on v0

--- a/solution.py
+++ b/solution.py
@@ -122,7 +122,8 @@
         lax.all_gather(out_weight, "grp", axis=1, tiled=True),
         preferred_element_type=jnp.float32,
     )
-    mixed = lax.psum(projected, "tp")
+    parts = lax.all_gather(projected, "tp")
+    mixed = jnp.sum(parts, axis=0)
     return mixed[None]
 
 

time: 216 us -> 186 us (0.86)
  waiting for transfers between devices: 65.8 us -> 36.1 us
    psum x1 -> x0, waiting for transfers between devices: 53.6 us -> none  [local(): mixed = lax.psum(projected, 'tp')]
    all_gather x0 -> x1, waiting for transfers between devices: none -> 23.9 us  [local(): parts = lax.all_gather(projected, 'tp')]
    unnamed x12 -> x11, local copies, waits for them, and re-layouts: 10.6 us -> 9.02 us
  transfers between devices with their start and end apart: 5 -> 5, of which waited for: 3 -> 3; matrix products, arithmetic and copies ran while one was open for 46% -> 54% of each run, Pallas kernels for 0% -> 0%
where the time goes in v1:
time: 186 us; the launch traced here: 185 us
  local copies, waits for them, and re-layouts  51.8 us (28%)
  other arithmetic  45 us (24%)
  waiting for transfers between devices  36.1 us (19%)
  blocking collectives  15.9 us (9%)
  between operations  14.3 us (8%)
  starting transfers between devices  13.2 us (7%)
  matrix products  8.29 us (4%)
    gather x8, local copies, waits for them, and re-layouts, local_block(): kv_pages[block_ids]  32.4 us
    all_gather x1, waiting for transfers between devices, local(): parts = lax.all_gather(projected, 'tp')  23.9 us
    unnamed x3, other arithmetic  20.7 us
    all_gather x1, blocking collectives, local(): gathered = lax.all_gather(queries, 'tp', axis=2, tiled=True)[0]  15.9 us
    select_n x8, other arithmetic, local_block(): block_lengths = jnp.where(block_slots < live_count, block_lengths, 0)  11 us
    unnamed x11, local copies, waits for them, and re-layouts  9.02 us
    all_to_all x1, waiting for transfers between devices, local(): lax.all_to_all(weighted[None], 'tp', split_axis=2, concat_axis=0, tiled=T...  7.53 us
    select_n x8, other arithmetic, local_block(): kv_pages[block_ids]  5.57 us
  transfers between devices with their start and end apart: 5, of which 3 were waited for; matrix products, arithmetic and copies ran while one was open for 54% of the time, Pallas kernels for 0%

profile of v1, /device:TPU:0, one launch (start us, length us, event | category | flops | bytes accessed | tf_op | source)
XLA Modules:
  0.0 185.3 jit_solution(13147229185468539076)
XLA Ops:
  6.5 0.7 all-gather.4.cloned.1.call-update
  7.9 15.9 %all_gather.12 = bf16[1,16,4096]{2,1,0:T(8,128)(2,1)S(1)} all-gather(bf16[1,16,512]{2,1,0:T(8,128)(2,1)} %param.12), channel_id=1, replica_groups=mesh['grp'=4,'tp'=8] {'tp'}, dimensions={2}, use_global_device_ids=true | all-gather | bytes 147456 | tf_op jit(solution)/shard_map/all_gather | solution.py:54
  23.9 65.7 %while.14 = (s32[]{:T(128)}, f32[16,4096]{1,0:T(8,128)S(1)}, f32[16,64]{1,0:T(8,128)S(1)}, f32[16,64]{1,0:T(8,128)S(1)}, s32[]{:T(128)}, /*index=5*/s32[]{:T(128...) while((s32[]{:T(128)}, f32[16,4096]{1,0:T(8,128)S(1)}, ...), condition=%wide.region_3.4_spmd, body=%wide.region_0.3_spmd.sunk | while | flops 8685212 | bytes 7998579 | solution.py:87
  24.0 1.4 compare_select_fusion.8
  26.4 4.0 %gather_fusion = bf16[32,16,1024]{2,1,0:T(8,128)(2,1)S(1)} fusion(bf16[256,16,1024]{2,1,0:T(8,128)(2,1)} %get-tuple-element.223, s32[1024]{0:T(1024)S(1)} %pad_clamp_fusion.2), kind=kCustom, calls=%fused_computation.clone.1 | custom fusion | bytes 2097280 | tf_op jit(solution)/shard_map/while/body/gather | solution.py:72
  32.1 1.4 compare_select_fusion.8
  34.5 4.5 %gather_fusion = bf16[32,16,1024]{2,1,0:T(8,128)(2,1)S(1)} fusion(bf16[256,16,1024]{2,1,0:T(8,128)(2,1)} %get-tuple-element.223, s32[1024]{0:T(1024)S(1)} %pad_clamp_fusion.2), kind=kCustom, calls=%fused_computation.clone.1 | custom fusion | bytes 2097280 | tf_op jit(solution)/shard_map/while/body/gather | solution.py:72
  40.7 1.4 compare_select_fusion.8
  43.2 4.0 %gather_fusion = bf16[32,16,1024]{2,1,0:T(8,128)(2,1)S(1)} fusion(bf16[256,16,1024]{2,1,0:T(8,128)(2,1)} %get-tuple-element.223, s32[1024]{0:T(1024)S(1)} %pad_clamp_fusion.2), kind=kCustom, calls=%fused_computation.clone.1 | custom fusion | bytes 2097280 | tf_op jit(solution)/shard_map/while/body/gather | solution.py:72
  48.9 1.4 compare_select_fusion.8
  51.3 4.0 %gather_fusion = bf16[32,16,1024]{2,1,0:T(8,128)(2,1)S(1)} fusion(bf16[256,16,1024]{2,1,0:T(8,128)(2,1)} %get-tuple-element.223, s32[1024]{0:T(1024)S(1)} %pad_clamp_fusion.2), kind=kCustom, calls=%fused_computation.clone.1 | custom fusion | bytes 2097280 | tf_op jit(solution)/shard_map/while/body/gather | solution.py:72
  57.0 1.4 compare_select_fusion.8
  59.4 4.0 %gather_fusion = bf16[32,16,1024]{2,1,0:T(8,128)(2,1)S(1)} fusion(bf16[256,16,1024]{2,1,0:T(8,128)(2,1)} %get-tuple-element.223, s32[1024]{0:T(1024)S(1)} %pad_clamp_fusion.2), kind=kCustom, calls=%fused_computation.clone.1 | custom fusion | bytes 2097280 | tf_op jit(solution)/shard_map/while/body/gather | solution.py:72
  65.2 1.4 compare_select_fusion.8
  67.6 4.0 %gather_fusion = bf16[32,16,1024]{2,1,0:T(8,128)(2,1)S(1)} fusion(bf16[256,16,1024]{2,1,0:T(8,128)(2,1)} %get-tuple-element.223, s32[1024]{0:T(1024)S(1)} %pad_clamp_fusion.2), kind=kCustom, calls=%fused_computation.clone.1 | custom fusion | bytes 2097280 | tf_op jit(solution)/shard_map/while/body/gather | solution.py:72
  73.3 1.4 compare_select_fusion.8
  75.7 4.0 %gather_fusion = bf16[32,16,1024]{2,1,0:T(8,128)(2,1)S(1)} fusion(bf16[256,16,1024]{2,1,0:T(8,128)(2,1)} %get-tuple-element.223, s32[1024]{0:T(1024)S(1)} %pad_clamp_fusion.2), kind=kCustom, calls=%fused_computation.clone.1 | custom fusion | bytes 2097280 | tf_op jit(solution)/shard_map/while/body/gather | solution.py:72
  81.5 1.4 compare_select_fusion.8
  83.9 4.0 %gather_fusion = bf16[32,16,1024]{2,1,0:T(8,128)(2,1)S(1)} fusion(bf16[256,16,1024]{2,1,0:T(8,128)(2,1)} %get-tuple-element.223, s32[1024]{0:T(1024)S(1)} %pad_clamp_fusion.2), kind=kCustom, calls=%fused_computation.clone.1 | custom fusion | bytes 2097280 | tf_op jit(solution)/shard_map/while/body/gather | solution.py:72
  91.6 4.6 %all-to-all-start.1 = ((f32[8,1,128]{2,1,0:T(1,128)}), f32[8,1,128]{2,1,0:T(1,128)S(1)}, u32[]{:S(2)}, u32[]{:S(2)}) async-start(f32[8,1,128]{2,1,0:T(1,128)} %reshape.170), calls=%async_computation.1 | async-start | bytes 8192 | tf_op jit(solution)/shard_map/all_to_all | solution.py:92
  96.4 0.7 reduce.3
  97.9 3.9 %all-to-all-done.1 = f32[8,1,128]{2,1,0:T(1,128)S(1)} async-done(((f32[8,1,128]{2,1,0:T(1,128)}), f32[8,1,128]{2,1,0:T(1,128)S(1)}, u32[]{:S(2)}, u32[]{:S(2)}) %all-to-all-start.1) | async-done | bytes 4128 | tf_op jit(solution)/shard_map/all_to_all | solution.py:92
  101.8 3.3 %all-to-all-start.2 = ((f32[8,1,128]{2,1,0:T(1,128)}), f32[8,1,128]{2,1,0:T(1,128)S(1)}, u32[]{:S(2)}, u32[]{:S(2)}) async-start(f32[8,1,128]{2,1,0:T(1,128)} %reshape.172), calls=%async_computation.2 | async-start | bytes 8192 | tf_op jit(solution)/shard_map/all_to_all | solution.py:93
  106.0 19.3 %reduce.1 = f32[4096,16]{1,0:T(8,128)} reduce(f32[4096,1,16]{2,1,0:T(1,128)S(1)} %bitcast.84, f32[]{:T(128)} %broadcast.132), dimensions={1}, to_apply=%bitcast.54.reduce_sub_computation | reduce | bytes 524292
  125.3 3.0 %reshape.168 = f32[8,1,8192]{2,1,0:T(1,128)} reshape(f32[4096,16]{1,0:T(8,128)} %reduce.1) | data formatting | bytes 524288
  128.3 5.0 %all-to-all-start = ((f32[8,1,8192]{2,1,0:T(1,128)}), f32[8,1,8192]{2,1,0:T(1,128)S(1)}, u32[]{:S(2)}, u32[]{:S(2)}) async-start(f32[8,1,8192]{2,1,0:T(1,128)} %reshape.168), calls=%async_computation | async-start | bytes 524288 | tf_op jit(solution)/shard_map/all_to_all | solution.py:91
  135.5 7.5 %all-to-all-done = f32[8,1,8192]{2,1,0:T(1,128)S(1)} async-done(((f32[8,1,8192]{2,1,0:T(1,128)}), f32[8,1,8192]{2,1,0:T(1,128)S(1)}, u32[]{:S(2)}, u32[]{:S(2)}) %all-to-all-start) | async-done | bytes 262176 | tf_op jit(solution)/shard_map/all_to_all | solution.py:91
  143.1 1.2 reduce.2
  144.3 3.9 %reshape.169 = f32[4096,1,16]{2,1,0:T(1,128)S(1)} reshape(f32[8,8192]{1,0:T(8,128)S(1)} %reduce.2) | data formatting | bytes 524288
  148.9 3.4 %fusion.15 = f32[16,2880]{1,0:T(8,128)} fusion(bf16[512,2880]{0,1:T(8,128)(2,1)} %all-gather.4.cloned.1.call-done, bf16[16,512]{1,0:T(8,128)(2,1)S(1)} %reshape.153, pred[16]{0:T(512)(128)(4,1)S(1)} %iota_compare_fusion.1), kind=kOutput, calls=%fused_computation.34 | convolution fusion | flops 47194112 | bytes 3149840 | tf_op jit(solution)/shard_map/dot_general | solution.py:120
  152.4 23.9 %all-gather.6.cloned.1.call-done = f32[128,2880]{1,0:T(8,128)} async-done(((f32[16,2880]{1,0:T(8,128)}), f32[128,2880]{1,0:T(8,128)}) %all-gather.6.cloned.1.call-update) | async-done | bytes 1474576 | tf_op jit(solution)/shard_map/all_gather | solution.py:125
  176.3 2.1 %reduce_sum.48 = f32[16,2880]{1,0:T(8,128)} reduce(f32[8,16,2880]{2,1,0:T(8,128)} %bitcast.86, f32[]{:T(128)} %constant.58.clone.1), dimensions={0}, to_apply=%region_8.9 | reduce | flops 322560 | bytes 1658884 | tf_op jit(solution)/shard_map/reduce_sum | solution.py:126
  (201 shorter events, 28.2 us)
Async XLA Ops:
  6.5 142.4 %all-gather.4.cloned.1.call-start = ((), (), s32[]{:S(2)}) async-start(), calls=%async_computation.3 | async-start | bytes 3686400 | tf_op jit(solution)/shard_map/all_gather | solution.py:122
  23.9 72.3 %copy-start.1 = (bf16[1,16,1024]{2,1,0:T(8,128)(2,1)S(1)}, bf16[1,16,1024]{2,1,0:T(8,128)(2,1)}, u32[]{:S(2)}) copy-start(bf16[1,16,1024]{2,1,0:T(8,128)(2,1)} %param.14) | copy-start | bytes 98308
  23.9 72.3 %copy-start = (bf16[1,16,512]{2,1,0:T(8,128)(2,1)S(1)}, bf16[1,16,512]{2,1,0:T(8,128)(2,1)}, u32[]{:S(2)}) copy-start(bf16[1,16,512]{2,1,0:T(8,128)(2,1)} %param.12) | copy-start | bytes 49156
  91.6 10.2 %all-to-all-start.1 = ((f32[8,1,128]{2,1,0:T(1,128)}), f32[8,1,128]{2,1,0:T(1,128)S(1)}, u32[]{:S(2)}, u32[]{:S(2)}) async-start(f32[8,1,128]{2,1,0:T(1,128)} %reshape.170), calls=%async_computation.1 | async-start | bytes 8192 | tf_op jit(solution)/shard_map/all_to_all | solution.py:92
  101.8 26.5 %all-to-all-start.2 = ((f32[8,1,128]{2,1,0:T(1,128)}), f32[8,1,128]{2,1,0:T(1,128)S(1)}, u32[]{:S(2)}, u32[]{:S(2)}) async-start(f32[8,1,128]{2,1,0:T(1,128)} %reshape.172), calls=%async_computation.2 | async-start | bytes 8192 | tf_op jit(solution)/shard_map/all_to_all | solution.py:93
  128.3 14.7 %all-to-all-start = ((f32[8,1,8192]{2,1,0:T(1,128)}), f32[8,1,8192]{2,1,0:T(1,128)S(1)}, u32[]{:S(2)}, u32[]{:S(2)}) async-start(f32[8,1,8192]{2,1,0:T(1,128)} %reshape.168), calls=%async_computation | async-start | bytes 524288 | tf_op jit(solution)/shard_map/all_to_all | solution.py:91
  133.4 42.9 %all-gather.6.cloned.1.call-start = ((), (), s32[]{:S(2)}) async-start(), calls=%async_computation.4 | async-start | bytes 1695744 | tf_op jit(solution)/shard_map/all_gather | solution.py:125
Sparse Core Ops, SparseCore 0:
  9.2 44.9 all-gather.3
  152.5 23.7 all-gather.5
